TPU v7x, 256 devices: a whole 4x4x8 slice. The times are simulated.
256 devices in a mesh: view: 16 (over z, core), blk: 16 (over y, x).
Axes of the slice: x: 4, y: 4, z: 8, core: 2. Of those that a mesh axis runs over, the one named last changes fastest.
Arguments:
- estimate: float32 [256, 128, 128], P('blk'), may hold values from 0.5 to 2
- images: bfloat16 [16, 256, 64, 128], P('view', 'blk'), may hold values from 0.5 to 2
- point_spread: float32 [8, 9, 7, 25], replicated, may hold values from 0.01 to 1
- covered: int32 [8, 16, 4], P(None, 'blk'), may hold values from 0 to 1, as said below
Outputs:
- estimate_next: float32 [256, 128, 128], P('blk')
Inputs may be any that keep to these rules, and one draw needn't show every extreme that they name: For each view and each block layer along the first dimension, the covered blocks are consecutive along the second dimension and at most 3; for every view some block layer has exactly 3.
All inputs are finite; a program needn't handle non-finite values.
Results may differ from a plain program's by a relative error of at most 0.0003.
Values may be sent and summed in bfloat16 or wider, within the bound.
A program may use at most 64 MiB of HBM per device.

v0:
```python
import jax
import jax.numpy as jnp
from jax import lax
from jax.sharding import PartitionSpec as P

BY = 32


def with_halo(cells, sides, width):
    for axis, dim in sides:
        count = lax.axis_size(axis)
        ends = count - 1
        head = lax.slice_in_dim(cells, 0, width, axis=dim)
        tail = lax.slice_in_dim(cells, cells.shape[dim] - width, cells.shape[dim], axis=dim)
        cells = jnp.concatenate(
            [
                lax.ppermute(tail, axis, [(i, (i + 1) % count) for i in range(ends)]),
                cells,
                lax.ppermute(head, axis, [((i + 1) % count, i) for i in range(ends)]),
            ],
            axis=dim,
        )
    return cells


def swapped(block, axis, stride):
    count = lax.axis_size(axis)
    route = []
    for low in range(count):
        high = low | 1 << stride
        if high != low and high < count:
            route += [(low, high), (high, low)]
    return lax.ppermute(block, axis, route)


def merged(part, axis, combine):
    gathered = lax.all_gather(part, axis)

    def take(source):
        return lax.dynamic_index_in_dim(gathered, source, 0, False)

    return lax.fori_loop(
        1, lax.axis_size(axis), lambda source, state: combine(state, take(source)), take(0)
    )


def band_table(kernel, depth):
    taps_x, taps_y, taps_z = kernel.shape
    rim_z = (taps_z - 1) // 2
    shape_three = (taps_z, depth, depth)
    offset = lax.broadcasted_iota(jnp.int32, shape_three, 1) - lax.broadcasted_iota(
        jnp.int32, shape_three, 2
    )
    onehot = (offset + rim_z == lax.broadcasted_iota(jnp.int32, shape_three, 0)).astype(
        jnp.bfloat16
    )
    banded = jnp.einsum("abt,tpz->abpz", kernel, onehot, preferred_element_type=jnp.float32).astype(
        jnp.bfloat16
    )
    return banded.reshape(taps_x, taps_y * depth, depth)


def convolve(padded_part, banded, rows_x, rows_y):
    taps_x = padded_part.shape[0] - rows_x + 1
    taps_y = padded_part.shape[1] - rows_y + 1
    columns = jnp.concatenate(
        [padded_part[:, step_y : step_y + rows_y, :] for step_y in range(taps_y)], axis=2
    )
    output = None
    for shift_x in range(taps_x):
        partial_sum = jnp.dot(
            columns[shift_x : shift_x + rows_x].reshape(rows_x * rows_y, -1),
            banded[shift_x],
            preferred_element_type=jnp.float32,
        )
        output = partial_sum if output is None else output + partial_sum
    return output.reshape(rows_x, rows_y, -1)


def local(estimate, images, point_spread, covered):
    slab_x, width_y, depth = estimate.shape
    share_w = images.shape[2]
    view_count, taps_x, taps_y, taps_z = point_spread.shape
    rim_x, rim_y, rim_z = ((taps_x - 1) // 2, (taps_y - 1) // 2, (taps_z - 1) // 2)
    shares = width_y // share_w
    share_blocks = share_w // BY
    group = lax.axis_index("view")
    view_id = group // shares
    part = group % shares
    y_start = part * share_w
    source = estimate.astype(jnp.bfloat16)
    rimmed = with_halo(source, (("blk", 0),), rim_x)
    padded = jnp.pad(rimmed, ((0, 0), (rim_y, rim_y), (0, 0)))
    spread = lax.dynamic_index_in_dim(point_spread, view_id, 0, keepdims=False)
    kernel = (spread / jnp.sum(spread)).astype(jnp.bfloat16)
    forward = band_table(kernel, depth)
    backward = band_table(kernel[::-1, ::-1, ::-1], depth)
    coverage_row = lax.dynamic_index_in_dim(covered[:, 0, :], view_id, 0, keepdims=False) > 0
    share_cover = lax.dynamic_slice_in_dim(coverage_row, part * share_blocks, share_blocks)
    cell_cover = jnp.repeat(share_cover, BY)[None, :, None]
    image = images[0]
    region = lax.dynamic_slice(
        padded, (0, y_start, 0), (slab_x + 2 * rim_x, share_w + 2 * rim_y, depth)
    )
    blurred = convolve(region, forward, slab_x, share_w)
    quotient = jnp.where(cell_cover, image.astype(jnp.float32) / blurred, 0.0).astype(jnp.bfloat16)
    rim_zeros = jnp.zeros((slab_x, rim_y, depth), jnp.bfloat16)
    edge_rows = jnp.where(part == 0, quotient[:, share_w - rim_y :, :], quotient[:, :rim_y, :])
    partner = swapped(edge_rows, "view", 0)
    lower_rim = jnp.where(part > 0, partner, rim_zeros)
    upper_rim = jnp.where(part < shares - 1, partner, rim_zeros)
    extended = jnp.concatenate([lower_rim, quotient, upper_rim], axis=1)
    quotient_rimmed = with_halo(extended, (("blk", 0),), rim_x)
    correction = convolve(quotient_rimmed, backward, slab_x, share_w)
    share_factor = jnp.where(cell_cover, correction, 1.0)
    n_view = lax.axis_size("view")
    step_x = slab_x // n_view
    rows = share_factor.reshape(n_view, step_x, share_w, depth)
    got = lax.all_to_all(rows, "view", 0, 0)
    got = got.reshape(n_view // shares, shares, step_x, share_w, depth)
    product_rows = jnp.prod(got, axis=0)
    product_rows = jnp.transpose(product_rows, (1, 0, 2, 3)).reshape(step_x, width_y, depth)
    mine = lax.dynamic_slice_in_dim(estimate, group * step_x, step_x, axis=0)
    return lax.all_gather(mine * product_rows, "view", axis=0, tiled=True)


def solution(mesh):
    in_specs = (P("blk", None, None), P("view", "blk", None, None), P(), P(None, "blk", None))
    out_specs = P("blk", None, None)
    return jax.shard_map(local, mesh=mesh, in_specs=in_specs, out_specs=out_specs, check_vma=False)
```

profile of v0, /device:TPU:1, one launch (start us, length us, event | category | flops | bytes accessed | tf_op | source)
XLA Modules:
  0.0 128.2 jit_solution(17272270914108477657)
XLA Ops:
  6.5 1.3 %convert_element_type.30 = bf16[16,128,128]{2,1,0:T(8,128)(2,1)S(1)} convert(f32[16,128,128]{2,1,0:T(8,128)} %param.4) | non-fusion elementwise | flops 262144 | bytes 1572864 | tf_op jit(solution)/shard_map/convert_element_type | solution.py:91
  7.9 4.0 %collective-permute-start = (bf16[4,128,128]{2,1,0:T(8,128)(2,1)S(1)}, bf16[4,128,128]{2,1,0:T(8,128)(2,1)S(1)}, u32[]{:S(2)}, u32[]{:S(2)}) collective-permute-start(bf16[4,128,128]{2,1,0:T(8,128)(2,1)S(1)} %get-tuple-element.44), channel_id=1, source_target_pairs={{0,1},{1,2},{2,3},{3,4},{4,5},{5,6},{6,7},{7,8},{8,9},{9,10},{10,1... | collective-permute-start | bytes 393224 | tf_op jit(solution)/shard_map/ppermute | solution.py:17
  11.8 1.3 %collective-permute-start.1 = (bf16[4,128,128]{2,1,0:T(8,128)(2,1)S(1)}, bf16[4,128,128]{2,1,0:T(8,128)(2,1)S(1)}, u32[]{:S(2)}, u32[]{:S(2)}) collective-permute-start(bf16[4,128,128]{2,1,0:T(8,128)(2,1)S(1)} %get-tuple-element.43), channel_id=1, source_target_pairs={{1,0},{2,1},{3,2},{4,3},{5,4},{6,5},{7,6},{8,7},{9,8},{10,9},{11,1... | collective-permute-start | bytes 393224 | tf_op jit(solution)/shard_map/ppermute | solution.py:19
  13.2 1.6 %fusion.30 = (f32[]{:T(128)}, f32[1,9,7,25]{3,0,2,1:T(1,128)S(1)}) fusion(f32[8,9,7,25]{3,0,2,1:T(8,128)} %param.6, s32[]{:T(128)S(6)} %select_n.62), kind=kLoop, calls=%fused_computation.73 | loop fusion | flops 1574 | bytes 12608 | tf_op jit(solution)/shard_map/reduce_sum | solution.py:95
  14.8 1.5 %fusion.5 = bf16[9,7,128,128]{3,1,2,0:T(8,128)(2,1)S(1)} fusion(f32[1,9,7,25]{3,0,2,1:T(1,128)S(1)} %get-tuple-element.6, f32[]{:T(128)} %get-tuple-element.5), kind=kOutput, calls=%fused_computation.4 | convolution fusion | flops 53873744 | bytes 2070688 | tf_op jit(solution)/shard_map/abt,tpz->abpz/dot_general | solution.py:57
  17.6 0.7 fusion.29
  19.9 3.2 %fusion.32 = (bf16[16,64,896]{2,1,0:T(8,128)(2,1)S(1)}, bf16[16,64,896]{2,1,0:T(8,128)(2,1)S(1)}, bf16[16,64,896]{2,1,0:T(8,128)(2,1)S(1)}, bf16[16,64,896]{2,1,...) fusion(bf16[24,64,896]{2,1,0:T(8,128)(2,1)S(1)} %slice_dynamic-, ...), kind=kLoop, calls=%fused_computation.75 | loop fusion | bytes 33030144 | tf_op jit(solution)/shard_map/slice | solution.py:72
  23.8 0.7 convolution_add_fusion.15
  24.4 0.6 convolution_add_fusion.14
  25.1 0.6 convolution_add_fusion.13
  25.7 0.6 convolution_add_fusion.12
  26.4 0.6 convolution_add_fusion.11
  27.0 0.6 convolution_add_fusion.10
  27.7 0.6 convolution_add_fusion.9
  28.4 0.7 convolution_add_fusion.8
  29.5 1.3 %collective-permute-start.2 = (bf16[16,3,128]{2,1,0:T(4,128)(2,1)S(1)}, bf16[16,3,128]{2,1,0:T(4,128)(2,1)S(1)}, u32[]{:S(2)}, u32[]{:S(2)}) collective-permute-start(bf16[16,3,128]{2,1,0:T(4,128)(2,1)S(1)} %slice_select_fusion), channel_id=1, source_target_pairs={{0,16},{16,0},{32,48},{48,32},{64,80},{80,64},{96,112},{112,96},{1... | collective-permute-start | bytes 36872 | tf_op jit(solution)/shard_map/ppermute | solution.py:33
  30.8 0.9 fusion.8
  31.8 1.3 %collective-permute-start.4 = (bf16[4,70,128]{2,1,0:T(8,128)(2,1)S(1)}, bf16[4,70,128]{2,1,0:T(8,128)(2,1)S(1)}, u32[]{:S(2)}, u32[]{:S(2)}) collective-permute-start(bf16[4,70,128]{2,1,0:T(8,128)(2,1)S(1)} %get-tuple-element.46), channel_id=1, source_target_pairs={{1,0},{2,1},{3,2},{4,3},{5,4},{6,5},{7,6},{8,7},{9,8},{10,9},{11,1... | collective-permute-start | bytes 215048 | tf_op jit(solution)/shard_map/ppermute | solution.py:19
  33.1 4.8 %collective-permute-start.3 = (bf16[4,70,128]{2,1,0:T(8,128)(2,1)S(1)}, bf16[4,70,128]{2,1,0:T(8,128)(2,1)S(1)}, u32[]{:S(2)}, u32[]{:S(2)}) collective-permute-start(bf16[4,70,128]{2,1,0:T(8,128)(2,1)S(1)} %get-tuple-element.45), channel_id=1, source_target_pairs={{0,1},{1,2},{2,3},{3,4},{4,5},{5,6},{6,7},{7,8},{8,9},{9,10},{10,1... | collective-permute-start | bytes 215048 | tf_op jit(solution)/shard_map/ppermute | solution.py:17
  40.3 3.2 %fusion.31 = (bf16[16,64,896]{2,1,0:T(8,128)(2,1)S(1)}, bf16[16,64,896]{2,1,0:T(8,128)(2,1)S(1)}, bf16[16,64,896]{2,1,0:T(8,128)(2,1)S(1)}, bf16[16,64,896]{2,1,...) fusion(bf16[24,64,896]{2,1,0:T(8,128)(2,1)S(1)} %slice_dynamic-, ...), kind=kLoop, calls=%fused_computation.74 | loop fusion | bytes 33030144 | tf_op jit(solution)/shard_map/slice | solution.py:72
  44.2 0.7 convolution_add_fusion.7
  44.8 0.6 convolution_add_fusion.6
  46.1 0.6 convolution_add_fusion.4
  46.8 0.6 convolution_add_fusion.3
  48.1 0.6 convolution_add_fusion.1
  48.8 0.6 convolution_add_fusion
  49.4 0.9 broadcast_select_fusion
  50.3 9.6 %all-to-all-start = ((f32[16,1,64,128]{3,2,1,0:T(8,128)}), f32[16,1,64,128]{3,2,1,0:T(8,128)S(1)}, u32[]{:S(2)}, u32[]{:S(2)}) async-start(f32[16,1,64,128]{3,2,1,0:T(8,128)} %broadcast_select_fusion), calls=%async_computation | async-start | bytes 1048576 | tf_op jit(solution)/shard_map/all_to_all | solution.py:119
  60.0 17.3 %all-to-all-done = f32[16,1,64,128]{3,2,1,0:T(8,128)S(1)} async-done(((f32[16,1,64,128]{3,2,1,0:T(8,128)}), f32[16,1,64,128]{3,2,1,0:T(8,128)S(1)}, u32[]{:S(2)}, u32[]{:S(2)}) %all-to-all-start) | async-done | bytes 524320 | tf_op jit(solution)/shard_map/all_to_all | solution.py:119
  77.3 1.5 %bitcast_multiply_fusion = f32[1,128,128]{2,1,0:T(8,128)} fusion(f32[16,128,128]{2,1,0:T(8,128)} %param.4, s32[]{:T(128)S(6)} %select_n.60, f32[1,128,128]{2,1,0:T(8,128)S(1)} %bitcast.144), kind=kLoop, calls=%fused_computation.59 | loop fusion | flops 16384 | bytes 196612 | tf_op jit(solution)/shard_map/mul | solution.py:124
  78.8 40.3 %all-gather.2.cloned.1.call-done = f32[16,128,128]{2,1,0:T(8,128)} async-done(((f32[1,128,128]{2,1,0:T(8,128)}), f32[16,128,128]{2,1,0:T(8,128)}) %all-gather.2.cloned.1.call-update) | async-done | bytes 1048592 | tf_op jit(solution)/shard_map/all_gather | solution.py:124
  119.1 2.3 %copy.70 = f32[16,128,128]{2,1,0:T(8,128)} copy(f32[16,128,128]{2,1,0:T(8,128)} %all-gather.2.cloned.1.call-done) | data formatting | bytes 2097152
  (62 shorter events, 8.3 us)
Async XLA Ops:
  7.9 10.5 %collective-permute-start = (bf16[4,128,128]{2,1,0:T(8,128)(2,1)S(1)}, bf16[4,128,128]{2,1,0:T(8,128)(2,1)S(1)}, u32[]{:S(2)}, u32[]{:S(2)}) collective-permute-start(bf16[4,128,128]{2,1,0:T(8,128)(2,1)S(1)} %get-tuple-element.44), channel_id=1, source_target_pairs={{0,1},{1,2},{2,3},{3,4},{4,5},{5,6},{6,7},{7,8},{8,9},{9,10},{10,1... | collective-permute-start | bytes 393224 | tf_op jit(solution)/shard_map/ppermute | solution.py:17
  11.8 6.6 %collective-permute-start.1 = (bf16[4,128,128]{2,1,0:T(8,128)(2,1)S(1)}, bf16[4,128,128]{2,1,0:T(8,128)(2,1)S(1)}, u32[]{:S(2)}, u32[]{:S(2)}) collective-permute-start(bf16[4,128,128]{2,1,0:T(8,128)(2,1)S(1)} %get-tuple-element.43), channel_id=1, source_target_pairs={{1,0},{2,1},{3,2},{4,3},{5,4},{6,5},{7,6},{8,7},{9,8},{10,9},{11,1... | collective-permute-start | bytes 393224 | tf_op jit(solution)/shard_map/ppermute | solution.py:19
  16.6 0.7 copy-start.1
  28.3 1.0 copy-start
  29.5 2.2 %collective-permute-start.2 = (bf16[16,3,128]{2,1,0:T(4,128)(2,1)S(1)}, bf16[16,3,128]{2,1,0:T(4,128)(2,1)S(1)}, u32[]{:S(2)}, u32[]{:S(2)}) collective-permute-start(bf16[16,3,128]{2,1,0:T(4,128)(2,1)S(1)} %slice_select_fusion), channel_id=1, source_target_pairs={{0,16},{16,0},{32,48},{48,32},{64,80},{80,64},{96,112},{112,96},{1... | collective-permute-start | bytes 36872 | tf_op jit(solution)/shard_map/ppermute | solution.py:33
  31.8 6.7 %collective-permute-start.4 = (bf16[4,70,128]{2,1,0:T(8,128)(2,1)S(1)}, bf16[4,70,128]{2,1,0:T(8,128)(2,1)S(1)}, u32[]{:S(2)}, u32[]{:S(2)}) collective-permute-start(bf16[4,70,128]{2,1,0:T(8,128)(2,1)S(1)} %get-tuple-element.46), channel_id=1, source_target_pairs={{1,0},{2,1},{3,2},{4,3},{5,4},{6,5},{7,6},{8,7},{9,8},{10,9},{11,1... | collective-permute-start | bytes 215048 | tf_op jit(solution)/shard_map/ppermute | solution.py:19
  33.1 6.0 %collective-permute-start.3 = (bf16[4,70,128]{2,1,0:T(8,128)(2,1)S(1)}, bf16[4,70,128]{2,1,0:T(8,128)(2,1)S(1)}, u32[]{:S(2)}, u32[]{:S(2)}) collective-permute-start(bf16[4,70,128]{2,1,0:T(8,128)(2,1)S(1)} %get-tuple-element.45), channel_id=1, source_target_pairs={{0,1},{1,2},{2,3},{3,4},{4,5},{5,6},{6,7},{7,8},{8,9},{9,10},{10,1... | collective-permute-start | bytes 215048 | tf_op jit(solution)/shard_map/ppermute | solution.py:17
  50.3 26.9 %all-to-all-start = ((f32[16,1,64,128]{3,2,1,0:T(8,128)}), f32[16,1,64,128]{3,2,1,0:T(8,128)S(1)}, u32[]{:S(2)}, u32[]{:S(2)}) async-start(f32[16,1,64,128]{3,2,1,0:T(8,128)} %broadcast_select_fusion), calls=%async_computation | async-start | bytes 1048576 | tf_op jit(solution)/shard_map/all_to_all | solution.py:119
  60.0 59.1 %all-gather.2.cloned.1.call-start = ((), (), s32[]{:S(2)}) async-start(), calls=%async_computation.1 | async-start | bytes 1114112 | tf_op jit(solution)/shard_map/all_gather | solution.py:124
Sparse Core Ops, SparseCore 0:
  78.9 40.0 all-gather.1
where the time goes:
time: 129 us; the launch traced here: 128 us
  waiting for transfers between devices  58.2 us (45%)
  starting transfers between devices  22.3 us (17%)
  matrix products  14 us (11%)
  between operations  14 us (11%)
  local copies, waits for them, and re-layouts  12.9 us (10%)
  other arithmetic  6.78 us (5%)
    all_gather x1, waiting for transfers between devices, local(): return lax.all_gather(mine * product_rows, 'view', axis=0, tiled=True)  40.3 us
    all_to_all x1, waiting for transfers between devices, local(): got = lax.all_to_all(rows, 'view', 0, 0)  17.3 us
    dot_general x18, matrix products, convolve(): jnp.dot(columns[shift_x:shift_x + rows_x].reshape(rows_x * rows_y, -1), b...  11.7 us
    all_to_all x1, starting transfers between devices, local(): got = lax.all_to_all(rows, 'view', 0, 0)  9.63 us
    ppermute x2, starting transfers between devices, with_halo(): lax.ppermute(tail, axis, [(i, (i + 1) % count) for i in range(ends)])  8.75 us
    slice x2, local copies, waits for them, and re-layouts, convolve(): columns[shift_x:shift_x + rows_x].reshape(rows_x * rows_y, -1)  6.38 us
    unnamed x17, local copies, waits for them, and re-layouts  4.82 us
    ppermute x2, starting transfers between devices, with_halo(): lax.ppermute(head, axis, [((i + 1) % count, i) for i in range(ends)])  2.58 us
  transfers between devices with their start and end apart: 7, of which 3 were waited for; matrix products, arithmetic and copies ran while one was open for 5% of the time, Pallas kernels for 0%

commit v1 on v0

--- a/solution.py
+++ b/solution.py
@@ -121,7 +121,9 @@
     product_rows = jnp.prod(got, axis=0)
     product_rows = jnp.transpose(product_rows, (1, 0, 2, 3)).reshape(step_x, width_y, depth)
     mine = lax.dynamic_slice_in_dim(estimate, group * step_x, step_x, axis=0)
-    return lax.all_gather(mine * product_rows, "view", axis=0, tiled=True)
+    return jnp.concatenate(
+        lax.all_to_all(jnp.stack(lax.axis_size("view") * [mine * product_rows], 0), "view", 0, 0), 0
+    )
 
 
 def solution(mesh):

time: 129 us -> 110 us (0.85)
  the two profiles are of different devices: /device:TPU:1 before, /device:TPU:25 now
where the time goes in v1:
time: 110 us
  blocking collectives  31.3 us (28%)
  starting transfers between devices  24.4 us (22%)
  waiting for transfers between devices  21.9 us (20%)
  matrix products  14 us (13%)
  local copies, waits for them, and re-layouts  11.7 us (11%)
  other arithmetic  6.15 us (6%)
    all_to_all x1, blocking collectives, local(): lax.all_to_all(jnp.stack(lax.axis_size('view') * [mine * product_rows], 0...  31.3 us
    all_to_all x1, waiting for transfers between devices, local(): got = lax.all_to_all(rows, 'view', 0, 0)  17.3 us
    dot_general x18, matrix products, convolve(): jnp.dot(columns[shift_x:shift_x + rows_x].reshape(rows_x * rows_y, -1), b...  11.6 us
    all_to_all x1, starting transfers between devices, local(): got = lax.all_to_all(rows, 'view', 0, 0)  10.2 us
    ppermute x2, starting transfers between devices, with_halo(): lax.ppermute(head, axis, [((i + 1) % count, i) for i in range(ends)])  7.67 us
    slice x2, local copies, waits for them, and re-layouts, convolve(): columns[shift_x:shift_x + rows_x].reshape(rows_x * rows_y, -1)  6.38 us
    ppermute x2, starting transfers between devices, with_halo(): lax.ppermute(tail, axis, [(i, (i + 1) % count) for i in range(ends)])  5.22 us
    ppermute x2, waiting for transfers between devices, with_halo(): lax.ppermute(tail, axis, [(i, (i + 1) % count) for i in range(ends)])  4.54 us
  transfers between devices with their start and end apart: 6, of which 2 were waited for; matrix products, arithmetic and copies ran while one was open for 6% of the time, Pallas kernels for 0%

profile of v1, /device:TPU:25, one launch (start us, length us, event | category | flops | bytes accessed | tf_op | source)
XLA Modules:
  0.0 110.0 jit_solution(11583578486269500536)
XLA Ops:
  0.0 1.3 %convert_element_type.30 = bf16[16,128,128]{2,1,0:T(8,128)(2,1)S(1)} convert(f32[16,128,128]{2,1,0:T(8,128)} %param.4) | non-fusion elementwise | flops 262144 | bytes 1572864 | tf_op jit(solution)/shard_map/convert_element_type | solution.py:91
  1.3 3.1 %collective-permute-start = (bf16[4,128,128]{2,1,0:T(8,128)(2,1)S(1)}, bf16[4,128,128]{2,1,0:T(8,128)(2,1)S(1)}, u32[]{:S(2)}, u32[]{:S(2)}) collective-permute-start(bf16[4,128,128]{2,1,0:T(8,128)(2,1)S(1)} %get-tuple-element.44), channel_id=1, source_target_pairs={{0,1},{1,2},{2,3},{3,4},{4,5},{5,6},{6,7},{7,8},{8,9},{9,10},{10,1... | collective-permute-start | bytes 393224 | tf_op jit(solution)/shard_map/ppermute | solution.py:17
  4.5 4.3 %collective-permute-start.1 = (bf16[4,128,128]{2,1,0:T(8,128)(2,1)S(1)}, bf16[4,128,128]{2,1,0:T(8,128)(2,1)S(1)}, u32[]{:S(2)}, u32[]{:S(2)}) collective-permute-start(bf16[4,128,128]{2,1,0:T(8,128)(2,1)S(1)} %get-tuple-element.43), channel_id=1, source_target_pairs={{1,0},{2,1},{3,2},{4,3},{5,4},{6,5},{7,6},{8,7},{9,8},{10,9},{11,1... | collective-permute-start | bytes 393224 | tf_op jit(solution)/shard_map/ppermute | solution.py:19
  8.8 1.6 %fusion.31 = (f32[]{:T(128)}, f32[1,9,7,25]{3,0,2,1:T(1,128)S(1)}) fusion(f32[8,9,7,25]{3,0,2,1:T(8,128)} %param.6, s32[]{:T(128)S(6)} %select_n.62), kind=kLoop, calls=%fused_computation.74 | loop fusion | flops 1574 | bytes 12608 | tf_op jit(solution)/shard_map/reduce_sum | solution.py:95
  10.4 1.5 %fusion.5 = bf16[9,7,128,128]{3,1,2,0:T(8,128)(2,1)S(1)} fusion(f32[1,9,7,25]{3,0,2,1:T(1,128)S(1)} %get-tuple-element.6, f32[]{:T(128)} %get-tuple-element.5), kind=kOutput, calls=%fused_computation.4 | convolution fusion | flops 53873744 | bytes 2070688 | tf_op jit(solution)/shard_map/abt,tpz->abpz/dot_general | solution.py:57
  13.2 0.7 fusion.30
  15.5 3.2 %fusion.33 = (bf16[16,64,896]{2,1,0:T(8,128)(2,1)S(1)}, bf16[16,64,896]{2,1,0:T(8,128)(2,1)S(1)}, bf16[16,64,896]{2,1,0:T(8,128)(2,1)S(1)}, bf16[16,64,896]{2,1,...) fusion(bf16[24,64,896]{2,1,0:T(8,128)(2,1)S(1)} %slice_dynamic-, ...), kind=kLoop, calls=%fused_computation.76 | loop fusion | bytes 33030144 | tf_op jit(solution)/shard_map/slice | solution.py:72
  18.7 0.6 fusion.37
  19.4 0.6 convolution_add_fusion.15
  20.0 0.6 convolution_add_fusion.14
  20.7 0.6 convolution_add_fusion.13
  21.3 0.6 convolution_add_fusion.12
  22.0 0.6 convolution_add_fusion.11
  22.6 0.6 convolution_add_fusion.10
  23.3 0.6 convolution_add_fusion.9
  24.0 0.7 convolution_add_fusion.8
  25.1 1.3 %collective-permute-start.2 = (bf16[16,3,128]{2,1,0:T(4,128)(2,1)S(1)}, bf16[16,3,128]{2,1,0:T(4,128)(2,1)S(1)}, u32[]{:S(2)}, u32[]{:S(2)}) collective-permute-start(bf16[16,3,128]{2,1,0:T(4,128)(2,1)S(1)} %slice_select_fusion), channel_id=1, source_target_pairs={{0,16},{16,0},{32,48},{48,32},{64,80},{80,64},{96,112},{112,96},{1... | collective-permute-start | bytes 36872 | tf_op jit(solution)/shard_map/ppermute | solution.py:33
  26.4 0.9 fusion.8
  27.4 3.4 %collective-permute-start.4 = (bf16[4,70,128]{2,1,0:T(8,128)(2,1)S(1)}, bf16[4,70,128]{2,1,0:T(8,128)(2,1)S(1)}, u32[]{:S(2)}, u32[]{:S(2)}) collective-permute-start(bf16[4,70,128]{2,1,0:T(8,128)(2,1)S(1)} %get-tuple-element.46), channel_id=1, source_target_pairs={{1,0},{2,1},{3,2},{4,3},{5,4},{6,5},{7,6},{8,7},{9,8},{10,9},{11,1... | collective-permute-start | bytes 215048 | tf_op jit(solution)/shard_map/ppermute | solution.py:19
  30.8 2.1 %collective-permute-start.3 = (bf16[4,70,128]{2,1,0:T(8,128)(2,1)S(1)}, bf16[4,70,128]{2,1,0:T(8,128)(2,1)S(1)}, u32[]{:S(2)}, u32[]{:S(2)}) collective-permute-start(bf16[4,70,128]{2,1,0:T(8,128)(2,1)S(1)} %get-tuple-element.45), channel_id=1, source_target_pairs={{0,1},{1,2},{2,3},{3,4},{4,5},{5,6},{6,7},{7,8},{8,9},{9,10},{10,1... | collective-permute-start | bytes 215048 | tf_op jit(solution)/shard_map/ppermute | solution.py:17
  33.5 4.5 %collective-permute-done.3 = bf16[4,70,128]{2,1,0:T(8,128)(2,1)S(1)} collective-permute-done((bf16[4,70,128]{2,1,0:T(8,128)(2,1)S(1)}, bf16[4,70,128]{2,1,0:T(8,128)(2,1)S(1)}, u32[]{:S(2)}, u32[]{:S(2)}) %collective-permute-start.3) | collective-permute-done | bytes 71712 | tf_op jit(solution)/shard_map/ppermute | solution.py:17
  39.3 3.2 %fusion.32 = (bf16[16,64,896]{2,1,0:T(8,128)(2,1)S(1)}, bf16[16,64,896]{2,1,0:T(8,128)(2,1)S(1)}, bf16[16,64,896]{2,1,0:T(8,128)(2,1)S(1)}, bf16[16,64,896]{2,1,...) fusion(bf16[24,64,896]{2,1,0:T(8,128)(2,1)S(1)} %slice_dynamic-, ...), kind=kLoop, calls=%fused_computation.75 | loop fusion | bytes 33030144 | tf_op jit(solution)/shard_map/slice | solution.py:72
  43.8 0.6 convolution_add_fusion.6
  44.4 0.6 convolution_add_fusion.5
  45.7 0.6 convolution_add_fusion.3
  47.7 0.6 convolution_add_fusion
  48.3 0.9 broadcast_select_fusion
  49.2 10.2 %all-to-all-start = ((f32[16,1,64,128]{3,2,1,0:T(8,128)}), f32[16,1,64,128]{3,2,1,0:T(8,128)S(1)}, u32[]{:S(2)}, u32[]{:S(2)}) async-start(f32[16,1,64,128]{3,2,1,0:T(8,128)} %broadcast_select_fusion), calls=%async_computation | async-start | bytes 1048576 | tf_op jit(solution)/shard_map/all_to_all | solution.py:119
  59.4 17.3 %all-to-all-done = f32[16,1,64,128]{3,2,1,0:T(8,128)S(1)} async-done(((f32[16,1,64,128]{3,2,1,0:T(8,128)}), f32[16,1,64,128]{3,2,1,0:T(8,128)S(1)}, u32[]{:S(2)}, u32[]{:S(2)}) %all-to-all-start) | async-done | bytes 524320 | tf_op jit(solution)/shard_map/all_to_all | solution.py:119
  76.8 0.9 fusion.23
  77.7 31.3 %all_to_all.10 = f32[16,1,128,128]{3,2,1,0:T(8,128)S(1)} all-to-all(f32[16,1,128,128]{3,2,1,0:T(8,128)S(1)} %stack.2), channel_id=1, replica_groups=mesh['view'=16,'blk'=16] {'view'}, dimensions={0} | all-to-all | bytes 2097152 | tf_op jit(solution)/shard_map/all_to_all | solution.py:125
  109.0 1.0 copy.70
  (61 shorter events, 8.3 us)
Async XLA Ops:
  1.3 12.7 %collective-permute-start = (bf16[4,128,128]{2,1,0:T(8,128)(2,1)S(1)}, bf16[4,128,128]{2,1,0:T(8,128)(2,1)S(1)}, u32[]{:S(2)}, u32[]{:S(2)}) collective-permute-start(bf16[4,128,128]{2,1,0:T(8,128)(2,1)S(1)} %get-tuple-element.44), channel_id=1, source_target_pairs={{0,1},{1,2},{2,3},{3,4},{4,5},{5,6},{6,7},{7,8},{8,9},{9,10},{10,1... | collective-permute-start | bytes 393224 | tf_op jit(solution)/shard_map/ppermute | solution.py:17
  4.5 9.6 %collective-permute-start.1 = (bf16[4,128,128]{2,1,0:T(8,128)(2,1)S(1)}, bf16[4,128,128]{2,1,0:T(8,128)(2,1)S(1)}, u32[]{:S(2)}, u32[]{:S(2)}) collective-permute-start(bf16[4,128,128]{2,1,0:T(8,128)(2,1)S(1)} %get-tuple-element.43), channel_id=1, source_target_pairs={{1,0},{2,1},{3,2},{4,3},{5,4},{6,5},{7,6},{8,7},{9,8},{10,9},{11,1... | collective-permute-start | bytes 393224 | tf_op jit(solution)/shard_map/ppermute | solution.py:19
  12.2 0.7 copy-start.1
  24.0 1.0 copy-start
  25.1 2.2 %collective-permute-start.2 = (bf16[16,3,128]{2,1,0:T(4,128)(2,1)S(1)}, bf16[16,3,128]{2,1,0:T(4,128)(2,1)S(1)}, u32[]{:S(2)}, u32[]{:S(2)}) collective-permute-start(bf16[16,3,128]{2,1,0:T(4,128)(2,1)S(1)} %slice_select_fusion), channel_id=1, source_target_pairs={{0,16},{16,0},{32,48},{48,32},{64,80},{80,64},{96,112},{112,96},{1... | collective-permute-start | bytes 36872 | tf_op jit(solution)/shard_map/ppermute | solution.py:33
  27.4 6.1 %collective-permute-start.4 = (bf16[4,70,128]{2,1,0:T(8,128)(2,1)S(1)}, bf16[4,70,128]{2,1,0:T(8,128)(2,1)S(1)}, u32[]{:S(2)}, u32[]{:S(2)}) collective-permute-start(bf16[4,70,128]{2,1,0:T(8,128)(2,1)S(1)} %get-tuple-element.46), channel_id=1, source_target_pairs={{1,0},{2,1},{3,2},{4,3},{5,4},{6,5},{7,6},{8,7},{9,8},{10,9},{11,1... | collective-permute-start | bytes 215048 | tf_op jit(solution)/shard_map/ppermute | solution.py:19
  30.8 7.2 %collective-permute-start.3 = (bf16[4,70,128]{2,1,0:T(8,128)(2,1)S(1)}, bf16[4,70,128]{2,1,0:T(8,128)(2,1)S(1)}, u32[]{:S(2)}, u32[]{:S(2)}) collective-permute-start(bf16[4,70,128]{2,1,0:T(8,128)(2,1)S(1)} %get-tuple-element.45), channel_id=1, source_target_pairs={{0,1},{1,2},{2,3},{3,4},{4,5},{5,6},{6,7},{7,8},{8,9},{9,10},{10,1... | collective-permute-start | bytes 215048 | tf_op jit(solution)/shard_map/ppermute | solution.py:17
  49.2 27.5 %all-to-all-start = ((f32[16,1,64,128]{3,2,1,0:T(8,128)}), f32[16,1,64,128]{3,2,1,0:T(8,128)S(1)}, u32[]{:S(2)}, u32[]{:S(2)}) async-start(f32[16,1,64,128]{3,2,1,0:T(8,128)} %broadcast_select_fusion), calls=%async_computation | async-start | bytes 1048576 | tf_op jit(solution)/shard_map/all_to_all | solution.py:119
